TPU v7x, 32 devices: a whole 2x2x4 slice. The times are simulated.
32 devices in a mesh: gx: 8 (over z, core), gy: 4 (over y, x).
Axes of the slice: x: 2, y: 2, z: 4, core: 2. Of those that a mesh axis runs over, the one named last changes fastest.
Arguments:
- base_state: float32 [3, 32, 32, 128], P(None, 'gx', 'gy'), may hold values from -5 to 5
- adjoint_block: float32 [32, 3, 32, 32, 128], P(None, None, 'gx', 'gy'), may hold values from -2500 to 2500
Outputs:
- q_block: float32 [32, 3, 32, 32, 128], P(None, None, 'gx', 'gy')
- r_factor: float32 [32, 32], replicated
All inputs are finite; a program needn't handle non-finite values.
Results may differ from a plain program's by a relative error of at most 0.00015.
Values sent between devices are 32-bit elements; how exact they have to be, the bound alone decides.
A program may use at most 64 MiB of HBM per device.

v0:
```python
import math

import jax
import jax.numpy as jnp
from jax import lax
from jax.sharding import PartitionSpec as P

ADVECT = 0.1
DIFFUSE = 0.08
DRIVE_SCALE = 0.25
WAVENUMBER = 4.0


def with_halo(value, sides, width):
    for axis, dim in sides:
        devices, length = (lax.axis_size(axis), value.shape[dim])
        up = [(i, (i + 1) % devices) for i in range(devices)]
        down = [(j, i) for i, j in up]
        last = lax.slice_in_dim(value, length - width, length, axis=dim)
        first = lax.slice_in_dim(value, 0, width, axis=dim)
        before = lax.ppermute(last, axis, up)
        after = lax.ppermute(first, axis, down)
        value = jnp.concatenate([before, value, after], axis=dim)
    return value


def advance(padded, column_index, ny_total):
    centre = padded[:, 1:-1, 1:-1, :]
    eastern = padded[:, 2:, 1:-1, :]
    western = padded[:, :-2, 1:-1, :]
    northern = padded[:, 1:-1, 2:, :]
    southern = padded[:, 1:-1, :-2, :]
    upward = jnp.roll(centre, -1, axis=3)
    downward = jnp.roll(centre, 1, axis=3)
    laplacian = eastern + western + northern + southern + upward + downward - 6.0 * centre
    advection = (
        centre[0:1] * (eastern - western)
        + centre[1:2] * (northern - southern)
        + centre[2:3] * (upward - downward)
    )
    phases = 2.0 * math.pi * WAVENUMBER * column_index.astype(jnp.float32) / float(ny_total)
    forcing = DRIVE_SCALE * jnp.sin(phases)
    nothing = jnp.zeros_like(forcing)
    driven = jnp.stack([forcing, nothing, nothing])[:, None, :, None]
    return centre + DIFFUSE * laplacian - ADVECT * advection + driven


def adjoint(base_ext, block_ext):
    inner = block_ext[:, :, 1:-1, 1:-1, :]
    base_inner = base_ext[:, 1:-1, 1:-1, :]
    base_east = base_ext[:, 2:, 1:-1, :]
    base_west = base_ext[:, :-2, 1:-1, :]
    base_north = base_ext[:, 1:-1, 2:, :]
    base_south = base_ext[:, 1:-1, :-2, :]
    block_east = block_ext[:, :, 2:, 1:-1, :]
    block_west = block_ext[:, :, :-2, 1:-1, :]
    block_north = block_ext[:, :, 1:-1, 2:, :]
    block_south = block_ext[:, :, 1:-1, :-2, :]
    carried = base_inner[2] * inner
    flux = base_east[0] * block_east - base_west[0] * block_west
    flux = flux + base_north[1] * block_north - base_south[1] * block_south
    flux = flux + jnp.roll(carried, -1, axis=-1) - jnp.roll(carried, 1, axis=-1)
    grad_x = base_east - base_west
    grad_y = base_north - base_south
    grad_z = jnp.roll(base_inner, -1, axis=3) - jnp.roll(base_inner, 1, axis=3)
    coupling = jnp.stack(
        [
            jnp.sum(inner * grad_x, axis=1),
            jnp.sum(inner * grad_y, axis=1),
            jnp.sum(inner * grad_z, axis=1),
        ],
        axis=1,
    )
    laplacian = (
        block_east
        + block_west
        + block_north
        + block_south
        + jnp.roll(inner, -1, axis=-1)
        + jnp.roll(inner, 1, axis=-1)
        - 6.0 * inner
    )
    return inner + ADVECT * (flux - coupling) + DIFFUSE * laplacian


def on_device(base_state, adjoint_block):
    vectors = adjoint_block.shape[0]
    width_y = base_state.shape[2]
    ny_total = width_y * lax.axis_size("gy")
    offset = lax.axis_index("gy") * width_y
    padded = with_halo(base_state, (("gx", 1), ("gy", 2)), 2)
    column_index = (offset + jnp.arange(-1, width_y + 1, dtype=jnp.int32)) % ny_total
    base_ext = advance(padded, column_index, ny_total)
    block_ext = with_halo(adjoint_block, (("gx", 2), ("gy", 3)), 1)
    updated = adjoint(base_ext, block_ext)
    flat = updated.reshape(vectors, -1)
    partial_gram = jnp.dot(
        flat, flat.T, precision=lax.Precision.HIGHEST, preferred_element_type=jnp.float32
    )
    entries = flat.shape[1] * lax.axis_size("gx") * lax.axis_size("gy")
    gram = lax.psum(partial_gram, ("gx", "gy")) / float(entries)
    lower = jnp.linalg.cholesky(gram)
    inverse = lax.linalg.triangular_solve(
        lower, jnp.eye(vectors, dtype=jnp.float32), left_side=True, lower=True
    )
    q_block = jnp.dot(
        inverse, flat, precision=lax.Precision.HIGHEST, preferred_element_type=jnp.float32
    ).reshape(updated.shape)
    return (q_block, lower.T)


def solution(mesh):
    in_specs = (P(None, "gx", "gy", None), P(None, None, "gx", "gy", None))
    out_specs = (P(None, None, "gx", "gy", None), P())
    return jax.shard_map(
        on_device, mesh=mesh, in_specs=in_specs, out_specs=out_specs, check_vma=False
    )
```

profile of v0, /device:TPU:0, one launch (start us, length us, event | category | flops | bytes accessed | tf_op | source)
XLA Modules:
  0.0 99.8 jit_solution(14381790056354557528)
XLA Ops:
  0.6 1.5 %fusion.34 = (f32[3,2,8,128]{3,2,1,0:T(8,128)}, f32[3,2,8,128]{3,2,1,0:T(8,128)}) fusion(f32[3,4,8,128]{3,2,1,0:T(8,128)} %param.2), kind=kLoop, calls=%fused_computation.78 | loop fusion | bytes 98304 | tf_op jit(solution)/shard_map/slice | solution.py:20
  2.1 4.5 %collective-permute-start.1 = (f32[3,2,8,128]{3,2,1,0:T(8,128)}, f32[3,2,8,128]{3,2,1,0:T(8,128)}, u32[]{:S(2)}, u32[]{:S(2)}) collective-permute-start(f32[3,2,8,128]{3,2,1,0:T(8,128)} %get-tuple-element.49), channel_id=1, source_target_pairs={{4,0},{8,4},{12,8},{16,12},{20,16},{24,20},{28,24},{0,28},{5,1},{9... | collective-permute-start | bytes 73736 | tf_op jit(solution)/shard_map/ppermute | solution.py:22
  6.7 2.1 %fusion.24 = (f32[32,3,1,8,128]{4,3,2,0,1:T(8,128)}, f32[32,3,1,8,128]{4,3,2,0,1:T(8,128)}) fusion(f32[32,3,4,8,128]{4,3,2,1,0:T(8,128)} %param.3), kind=kLoop, calls=%fused_computation.68 | loop fusion | bytes 1572864 | tf_op jit(solution)/shard_map/slice | solution.py:20
  8.7 3.5 %collective-permute-start.4 = (f32[32,3,1,8,128]{4,3,2,0,1:T(8,128)}, f32[32,3,1,8,128]{4,3,2,0,1:T(8,128)S(1)}, u32[]{:S(2)}, u32[]{:S(2)}) collective-permute-start(f32[32,3,1,8,128]{4,3,2,0,1:T(8,128)} %get-tuple-element.17), channel_id=1, source_target_pairs={{4,0},{8,4},{12,8},{16,12},{20,16},{24,20},{28,24},{0,28},{5,1},{9... | collective-permute-start | bytes 1179656 | tf_op jit(solution)/shard_map/ppermute | solution.py:22
  12.3 1.7 %fusion.25 = (f32[32,3,4,8,1]{4,3,2,0,1:T(8,128)S(1)}, f32[32,3,4,8,1]{4,3,2,0,1:T(8,128)}) fusion(f32[32,3,4,8,128]{4,3,2,1,0:T(8,128)S(1)} %copy-done), kind=kLoop, calls=%fused_computation.69 | loop fusion | bytes 3170304 | tf_op jit(solution)/shard_map/jit(_roll_static)/slice | solution.py:80
  14.0 2.2 %fusion.26 = (f32[32,3,4,8,127]{4,3,2,0,1:T(8,128)}, f32[32,3,4,8,127]{4,3,2,0,1:T(8,128)}) fusion(f32[32,3,4,8,128]{4,3,2,1,0:T(8,128)S(1)} %copy-done), kind=kLoop, calls=%fused_computation.70 | loop fusion | bytes 6266880 | tf_op jit(solution)/shard_map/jit(_roll_static)/slice | solution.py:80
  16.2 0.7 constant_dynamic-update-slice_fusion.2
  16.9 0.8 constant_dynamic-update-slice_fusion.1
  17.8 0.7 constant_dynamic-update-slice_fusion
  18.5 1.5 %collective-permute-start.2 = (f32[3,8,2,128]{3,2,1,0:T(2,128)S(1)}, f32[3,8,2,128]{3,2,1,0:T(2,128)S(1)}, u32[]{:S(2)}, u32[]{:S(2)}) collective-permute-start(f32[3,8,2,128]{3,2,1,0:T(2,128)S(1)} %get-tuple-element.47), channel_id=1, source_target_pairs={{0,1},{1,2},{2,3},{3,0},{4,5},{5,6},{6,7},{7,4},{8,9},{9,10},{10,1... | collective-permute-start | bytes 73736 | tf_op jit(solution)/shard_map/ppermute | solution.py:21
  20.1 1.4 %collective-permute-start.3 = (f32[3,8,2,128]{3,2,1,0:T(2,128)S(1)}, f32[3,8,2,128]{3,2,1,0:T(2,128)S(1)}, u32[]{:S(2)}, u32[]{:S(2)}) collective-permute-start(f32[3,8,2,128]{3,2,1,0:T(2,128)S(1)} %get-tuple-element.48), channel_id=1, source_target_pairs={{1,0},{2,1},{3,2},{0,3},{5,4},{6,5},{7,6},{4,7},{9,8},{10,9},{11,1... | collective-permute-start | bytes 73736 | tf_op jit(solution)/shard_map/ppermute | solution.py:22
  21.5 0.1 fusion.21
  21.5 0.1 copy.62
  21.7 1.6 %collective-permute-done.2 = f32[3,8,2,128]{3,2,1,0:T(2,128)S(1)} collective-permute-done((f32[3,8,2,128]{3,2,1,0:T(2,128)S(1)}, f32[3,8,2,128]{3,2,1,0:T(2,128)S(1)}, u32[]{:S(2)}, u32[]{:S(2)}) %collective-permute-start.2) | collective-permute-done | bytes 24608 | tf_op jit(solution)/shard_map/ppermute | solution.py:21
  23.3 0.6 collective-permute-done.3
  24.0 0.1 fusion.29
  24.1 0.1 fusion.30
  24.2 0.2 subtract_add_fusion
  24.4 0.1 fusion.31
  24.5 0.1 fusion.32
  24.5 0.1 slice_subtract_fusion
  24.6 0.5 multiply_reduce_fusion.2
  25.2 1.0 %constant_dynamic-update-slice_fusion.5 = f32[32,3,6,8,128]{4,3,2,0,1:T(8,128)S(1)} fusion(f32[32,3,1,8,128]{4,3,2,0,1:T(8,128)} %collective-permute-done.5), kind=kLoop, calls=%fused_computation.55 | loop fusion | bytes 786432
  26.2 0.3 constant_dynamic-update-slice_fusion.4
  26.6 0.4 fusion.23
  27.1 2.4 %collective-permute-start.7 = (f32[32,3,6,1,128]{4,0,3,2,1:T(8,128)S(1)}, f32[32,3,6,1,128]{4,0,3,2,1:T(8,128)S(1)}, u32[]{:S(2)}, u32[]{:S(2)}) collective-permute-start(f32[32,3,6,1,128]{4,0,3,2,1:T(8,128)S(1)} %copy.59), channel_id=1, source_target_pairs={{0,1},{1,2},{2,3},{3,0},{4,5},{5,6},{6,7},{7,4},{8,9},{9,10},{10,1... | collective-permute-start | bytes 884744 | tf_op jit(solution)/shard_map/ppermute | solution.py:21
  29.5 0.5 collective-permute-start.6
  30.0 0.6 fusion.28
  30.6 0.6 fusion.27
  31.2 4.8 %collective-permute-done.7 = f32[32,3,6,1,128]{4,0,3,2,1:T(8,128)S(1)} collective-permute-done((f32[32,3,6,1,128]{4,0,3,2,1:T(8,128)S(1)}, f32[32,3,6,1,128]{4,0,3,2,1:T(8,128)S(1)}, u32[]{:S(2)}, u32[]{:S(2)}) %collective-permute-start.7) | collective-permute-done | bytes 294944 | tf_op jit(solution)/shard_map/ppermute | solution.py:21
  36.0 0.3 copy.60
  36.3 2.9 %collective-permute-done.6 = f32[32,3,6,1,128]{4,0,3,2,1:T(8,128)S(1)} collective-permute-done((f32[32,3,6,1,128]{4,0,3,2,1:T(8,128)S(1)}, f32[32,3,6,1,128]{4,0,3,2,1:T(8,128)S(1)}, u32[]{:S(2)}, u32[]{:S(2)}) %collective-permute-start.6) | collective-permute-done | bytes 294944 | tf_op jit(solution)/shard_map/ppermute | solution.py:22
  39.2 0.3 copy.58
  39.6 3.9 %fusion.4 = f32[32,3,4,8,128]{4,3,2,0,1:T(8,128)S(1)} fusion(f32[32,3,4,8,128]{4,3,2,0,1:T(8,128)S(1)} %copy.62, f32[32,3,4,8,1]{4,3,2,0,1:T(8,128)S(1)} %get-tuple-element.26, f32[32,3,4,8,127]{4,3,2,0,1:T(8,128)S(1)} %get-tuple-element.28, f32[32,3,4,8,127]{4,3,2,0,1:T(8,128)S(1)} %get-tuple-element.27, f32[32,3,4,8,1]{4,3,2,0,1:T(8,128)S(1)} %get-tuple-element.25, ...), kind=kLoop, calls=%fused_computation.10 | loop fusion | flops 12189696 | bytes 14811136 | tf_op jit(solution)/shard_map/add | solution.py:83
  43.5 2.2 %fusion.12 = f32[32,32]{0,1:T(8,128)S(1)} fusion(f32[32,3,4,8,128]{4,3,2,0,1:T(8,128)S(1)} %fusion.4), kind=kOutput, calls=%fused_computation.22 | convolution fusion | flops 150994944 | bytes 1576960 | tf_op jit(solution)/shard_map/dot_general | solution.py:97
  45.6 0.1 copy.72
  45.8 40.7 %psum.7 = f32[32,32]{0,1:T(8,128)S(1)} all-reduce(f32[32,32]{0,1:T(8,128)S(1)} %fusion.12), channel_id=1, replica_groups=mesh['gx'=8,'gy'=4] {'gx','gy'}, use_global_device_ids=true, to_apply=%region_3.4 | all-reduce | flops 1024 | bytes 8192 | tf_op jit(solution)/shard_map/psum | solution.py:101
  86.5 0.9 copy.96
  87.4 0.3 copy.80
  87.7 0.1 copy.71
  87.8 2.9 %cholesky.17 = f32[32,32]{1,0:T(8,128)S(1)} custom-call(f32[32,32]{1,0:T(8,128)S(1)} %fusion.16), custom_call_target="Cholesky" | custom-call | tf_op jit(solution)/shard_map/jit(cholesky)/cholesky | solution.py:102
  90.8 0.6 compare_reduce_fusion
  91.4 0.7 fusion.17
  92.1 0.7 copy.75
  92.7 2.4 %custom-call.6 = f32[1,32,32]{1,2,0:T(8,128)S(1)} custom-call(f32[1,32,32]{2,1,0:T(8,128)S(1)} %get-tuple-element.52), custom_call_target="InvertDiagBlocksLowerTriangular" | custom-call | tf_op jit(solution)/shard_map/triangular_solve | solution.py:103
  95.2 0.2 convolution_bitcast_fusion
  95.4 2.3 %fusion.8 = f32[32,3,4,8,128]{4,0,3,2,1:T(8,128)S(1)} fusion(f32[32,32,1,1,1]{1,0,4,3,2:T(8,128)S(1)} %convolution_bitcast_fusion, f32[3,4,8,128,32]{3,2,1,0,4:T(8,128)S(1)} %bitcast.50), kind=kOutput, calls=%fused_computation.15 | convolution fusion | flops 150994944 | bytes 3149824 | tf_op jit(solution)/shard_map/dot_general | solution.py:106
  97.7 2.1 %copy.74 = f32[32,3,4,8,128]{4,3,2,1,0:T(8,128)} copy(f32[32,3,4,8,128]{4,0,3,2,1:T(8,128)S(1)} %fusion.8) | data formatting | bytes 3145728
  (25 shorter events, 0.3 us)
Async XLA Ops:
  0.6 11.6 %copy-start = (f32[32,3,4,8,128]{4,3,2,1,0:T(8,128)S(1)}, f32[32,3,4,8,128]{4,3,2,1,0:T(8,128)}, u32[]{:S(2)}) copy-start(f32[32,3,4,8,128]{4,3,2,1,0:T(8,128)} %param.3) | copy-start | bytes 4718596
  2.1 15.6 %collective-permute-start.1 = (f32[3,2,8,128]{3,2,1,0:T(8,128)}, f32[3,2,8,128]{3,2,1,0:T(8,128)}, u32[]{:S(2)}, u32[]{:S(2)}) collective-permute-start(f32[3,2,8,128]{3,2,1,0:T(8,128)} %get-tuple-element.49), channel_id=1, source_target_pairs={{4,0},{8,4},{12,8},{16,12},{20,16},{24,20},{28,24},{0,28},{5,1},{9... | collective-permute-start | bytes 73736 | tf_op jit(solution)/shard_map/ppermute | solution.py:22
  6.7 9.6 %collective-permute-start = (f32[3,2,8,128]{3,2,1,0:T(8,128)}, f32[3,2,8,128]{3,2,1,0:T(8,128)}, u32[]{:S(2)}, u32[]{:S(2)}) collective-permute-start(f32[3,2,8,128]{3,2,1,0:T(8,128)} %get-tuple-element.50), channel_id=1, source_target_pairs={{0,4},{4,8},{8,12},{12,16},{16,20},{20,24},{24,28},{28,0},{1,5},{5... | collective-permute-start | bytes 73736 | tf_op jit(solution)/shard_map/ppermute | solution.py:21
  8.7 17.9 %collective-permute-start.4 = (f32[32,3,1,8,128]{4,3,2,0,1:T(8,128)}, f32[32,3,1,8,128]{4,3,2,0,1:T(8,128)S(1)}, u32[]{:S(2)}, u32[]{:S(2)}) collective-permute-start(f32[32,3,1,8,128]{4,3,2,0,1:T(8,128)} %get-tuple-element.17), channel_id=1, source_target_pairs={{4,0},{8,4},{12,8},{16,12},{20,16},{24,20},{28,24},{0,28},{5,1},{9... | collective-permute-start | bytes 1179656 | tf_op jit(solution)/shard_map/ppermute | solution.py:22
  12.3 13.0 %collective-permute-start.5 = (f32[32,3,1,8,128]{4,3,2,0,1:T(8,128)}, f32[32,3,1,8,128]{4,3,2,0,1:T(8,128)}, u32[]{:S(2)}, u32[]{:S(2)}) collective-permute-start(f32[32,3,1,8,128]{4,3,2,0,1:T(8,128)} %get-tuple-element.18), channel_id=1, source_target_pairs={{0,4},{4,8},{8,12},{12,16},{16,20},{20,24},{24,28},{28,0},{1,5},{5... | collective-permute-start | bytes 1179656 | tf_op jit(solution)/shard_map/ppermute | solution.py:21
  18.5 4.8 %collective-permute-start.2 = (f32[3,8,2,128]{3,2,1,0:T(2,128)S(1)}, f32[3,8,2,128]{3,2,1,0:T(2,128)S(1)}, u32[]{:S(2)}, u32[]{:S(2)}) collective-permute-start(f32[3,8,2,128]{3,2,1,0:T(2,128)S(1)} %get-tuple-element.47), channel_id=1, source_target_pairs={{0,1},{1,2},{2,3},{3,0},{4,5},{5,6},{6,7},{7,4},{8,9},{9,10},{10,1... | collective-permute-start | bytes 73736 | tf_op jit(solution)/shard_map/ppermute | solution.py:21
  20.1 3.8 %collective-permute-start.3 = (f32[3,8,2,128]{3,2,1,0:T(2,128)S(1)}, f32[3,8,2,128]{3,2,1,0:T(2,128)S(1)}, u32[]{:S(2)}, u32[]{:S(2)}) collective-permute-start(f32[3,8,2,128]{3,2,1,0:T(2,128)S(1)} %get-tuple-element.48), channel_id=1, source_target_pairs={{1,0},{2,1},{3,2},{0,3},{5,4},{6,5},{7,6},{4,7},{9,8},{10,9},{11,1... | collective-permute-start | bytes 73736 | tf_op jit(solution)/shard_map/ppermute | solution.py:22
  27.1 9.0 %collective-permute-start.7 = (f32[32,3,6,1,128]{4,0,3,2,1:T(8,128)S(1)}, f32[32,3,6,1,128]{4,0,3,2,1:T(8,128)S(1)}, u32[]{:S(2)}, u32[]{:S(2)}) collective-permute-start(f32[32,3,6,1,128]{4,0,3,2,1:T(8,128)S(1)} %copy.59), channel_id=1, source_target_pairs={{0,1},{1,2},{2,3},{3,0},{4,5},{5,6},{6,7},{7,4},{8,9},{9,10},{10,1... | collective-permute-start | bytes 884744 | tf_op jit(solution)/shard_map/ppermute | solution.py:21
  29.5 9.7 %collective-permute-start.6 = (f32[32,3,6,1,128]{4,0,3,2,1:T(8,128)S(1)}, f32[32,3,6,1,128]{4,0,3,2,1:T(8,128)S(1)}, u32[]{:S(2)}, u32[]{:S(2)}) collective-permute-start(f32[32,3,6,1,128]{4,0,3,2,1:T(8,128)S(1)} %copy.57), channel_id=1, source_target_pairs={{1,0},{2,1},{3,2},{0,3},{5,4},{6,5},{7,6},{4,7},{9,8},{10,9},{11,1... | collective-permute-start | bytes 884744 | tf_op jit(solution)/shard_map/ppermute | solution.py:22
  30.6 8.9 %copy-start.1 = (f32[32,3,4,8,1]{4,3,2,0,1:T(8,128)S(1)}, f32[32,3,4,8,1]{4,3,2,0,1:T(8,128)}, u32[]{:S(2)}) copy-start(f32[32,3,4,8,1]{4,3,2,0,1:T(8,128)} %get-tuple-element.22) | copy-start | bytes 36868
  30.6 8.9 %copy-start.2 = (f32[32,3,4,8,127]{4,3,2,0,1:T(8,128)S(1)}, f32[32,3,4,8,127]{4,3,2,0,1:T(8,128)}, u32[]{:S(2)}) copy-start(f32[32,3,4,8,127]{4,3,2,0,1:T(8,128)} %get-tuple-element.23) | copy-start | bytes 4681732
  30.6 8.9 %copy-start.3 = (f32[32,3,4,8,127]{4,3,2,0,1:T(8,128)S(1)}, f32[32,3,4,8,127]{4,3,2,0,1:T(8,128)}, u32[]{:S(2)}) copy-start(f32[32,3,4,8,127]{4,3,2,0,1:T(8,128)} %get-tuple-element.24) | copy-start | bytes 4681732
where the time goes:
time: 100 us; the launch traced here: 99.8 us
  blocking collectives  40.7 us (41%)
  local copies, waits for them, and re-layouts  17.7 us (18%)
  starting transfers between devices  14 us (14%)
  other arithmetic  11.8 us (12%)
  waiting for transfers between devices  9.93 us (10%)
  matrix products  4.68 us (5%)
    psum x1, blocking collectives, on_device(): gram = lax.psum(partial_gram, ('gx', 'gy')) / float(entries)  40.7 us
    ppermute x4, starting transfers between devices, with_halo(): after = lax.ppermute(first, axis, down)  10 us
    unnamed x16, local copies, waits for them, and re-layouts  6.64 us
    ppermute x4, waiting for transfers between devices, with_halo(): before = lax.ppermute(last, axis, up)  6.43 us
    ppermute x4, starting transfers between devices, with_halo(): before = lax.ppermute(last, axis, up)  3.99 us
    slice x2, local copies, waits for them, and re-layouts, adjoint(): jnp.roll(inner, 1, axis=-1)  3.94 us
    slice x4, local copies, waits for them, and re-layouts, with_halo(): first = lax.slice_in_dim(value, 0, width, axis=dim)  3.93 us
    add x1, other arithmetic, adjoint(): return inner + ADVECT * (flux - coupling) + DIFFUSE * laplacian  3.88 us
  transfers between devices with their start and end apart: 8, of which 4 were waited for; matrix products, arithmetic and copies ran while one was open for 13% of the time, Pallas kernels for 0%

commit v1 on v0

--- a/solution.py
+++ b/solution.py
@@ -1,14 +1,128 @@
+import functools
 import math
 
 import jax
 import jax.numpy as jnp
 from jax import lax
+from jax.experimental import pallas as pl
+from jax.experimental.pallas import tpu as pltpu
 from jax.sharding import PartitionSpec as P
 
 ADVECT = 0.1
 DIFFUSE = 0.08
 DRIVE_SCALE = 0.25
 WAVENUMBER = 4.0
+MESH = pl.DeviceIdType.MESH
+
+
+def positions(nx, ny):
+    gx, gy = lax.axis_index("gx"), lax.axis_index("gy")
+    return (gx, gy, lax.rem(gx, 2) * ny + gy, gx // 2)
+
+
+def plane_peer(nx, ny, step):
+    gx, gy, mine, line = positions(nx, ny)
+    place = lax.rem(mine + step, 2 * ny)
+    return (line * 2 + place // ny, lax.rem(place, ny))
+
+
+def line_peer(nx, ny, step):
+    gx, gy, mine, line = positions(nx, ny)
+    return (lax.rem(line + step, nx // 2) * 2 + lax.rem(gx, 2), gy)
+
+
+def total_gram(nx, ny, plane, line, send_a, recv_a, send_b, recv_b):
+    gx, gy, mine, place = positions(nx, ny)
+    members, planes = 2 * ny, nx // 2
+
+    def hop_a(step):
+        return pltpu.make_async_remote_copy(
+            plane.at[mine], plane.at[mine], send_a.at[step], recv_a.at[step],
+            device_id=plane_peer(nx, ny, step), device_id_type=MESH)
+
+    def hop_b(step):
+        return pltpu.make_async_remote_copy(
+            line.at[place], line.at[place], send_b.at[step], recv_b.at[step],
+            device_id=line_peer(nx, ny, step), device_id_type=MESH)
+
+    for step in range(1, members):
+        hop_a(step).start()
+    for step in range(1, members):
+        hop_a(step).wait_recv()
+    total = plane[0]
+    for i in range(1, members):
+        total = total + plane[i]
+    line[place] = total
+    for step in range(1, planes):
+        hop_b(step).start()
+    for step in range(1, planes):
+        hop_b(step).wait_recv()
+    total = line[0]
+    for i in range(1, planes):
+        total = total + line[i]
+    for step in range(1, members):
+        hop_a(step).wait_send()
+    for step in range(1, planes):
+        hop_b(step).wait_send()
+    return total
+
+
+def eliminate(gram):
+    size = gram.shape[0]
+    rows = lax.broadcasted_iota(jnp.int32, (size, size), 0)
+    cols = lax.broadcasted_iota(jnp.int32, (size, size), 1)
+    left, right = gram, (rows == cols).astype(jnp.float32)
+    row = lax.broadcasted_iota(jnp.int32, (size, 1), 0)
+    m = jnp.concatenate([left, right], axis=1)
+    pivots = jnp.zeros((size, 1), jnp.float32)
+    for k in range(size):
+        pivot_row = m[k : k + 1, :]
+        pivot = pivot_row[:, k : k + 1]
+        column = m[:, k : k + 1]
+        pivots = jnp.where(row == k, pivot, pivots)
+        factor = jnp.where(row > k, column / pivot, 0.0)
+        m = m - factor * pivot_row
+    m = m * lax.rsqrt(pivots)
+    upper = jnp.where(cols >= rows, m[:, :size], 0.0)
+    return upper, m[:, size:]
+
+
+def meet(nx, ny):
+    barrier = pltpu.get_barrier_semaphore()
+    for step in range(1, 2 * ny):
+        pl.semaphore_signal(barrier, inc=1, device_id=plane_peer(nx, ny, step), device_id_type=MESH)
+    for step in range(1, nx // 2):
+        pl.semaphore_signal(barrier, inc=1, device_id=line_peer(nx, ny, step), device_id_type=MESH)
+    pl.semaphore_wait(barrier, 2 * ny + nx // 2 - 2)
+
+
+def gram_kernel(nx, ny, entries, part, upper, inverse, plane, line, send_a, recv_a, send_b, recv_b):
+    meet(nx, ny)
+    gx, gy, mine, place = positions(nx, ny)
+    plane[mine] = part[...]
+    gram = total_gram(nx, ny, plane, line, send_a, recv_a, send_b, recv_b) / entries
+    upper[...], inverse[...] = eliminate(gram)
+
+
+def factor_of(partial_gram, nx, ny, entries):
+    size = partial_gram.shape[0]
+    square = jax.ShapeDtypeStruct((size, size), jnp.float32)
+    vmem = pl.BlockSpec(memory_space=pltpu.VMEM)
+    return pl.pallas_call(
+        functools.partial(gram_kernel, nx, ny, entries),
+        out_shape=(square, square),
+        in_specs=[vmem],
+        out_specs=(vmem, vmem),
+        scratch_shapes=[
+            pltpu.VMEM((2 * ny, size, size), jnp.float32),
+            pltpu.VMEM((nx // 2, size, size), jnp.float32),
+            pltpu.SemaphoreType.DMA((2 * ny,)),
+            pltpu.SemaphoreType.DMA((2 * ny,)),
+            pltpu.SemaphoreType.DMA((nx // 2,)),
+            pltpu.SemaphoreType.DMA((nx // 2,)),
+        ],
+        compiler_params=pltpu.CompilerParams(collective_id=0, has_side_effects=True),
+    )(partial_gram)
 
 
 def with_halo(value, sides, width):
@@ -98,15 +212,13 @@
         flat, flat.T, precision=lax.Precision.HIGHEST, preferred_element_type=jnp.float32
     )
     entries = flat.shape[1] * lax.axis_size("gx") * lax.axis_size("gy")
-    gram = lax.psum(partial_gram, ("gx", "gy")) / float(entries)
-    lower = jnp.linalg.cholesky(gram)
-    inverse = lax.linalg.triangular_solve(
-        lower, jnp.eye(vectors, dtype=jnp.float32), left_side=True, lower=True
+    upper, inverse = factor_of(
+        partial_gram, lax.axis_size("gx"), lax.axis_size("gy"), float(entries)
     )
     q_block = jnp.dot(
         inverse, flat, precision=lax.Precision.HIGHEST, preferred_element_type=jnp.float32
     ).reshape(updated.shape)
-    return (q_block, lower.T)
+    return (q_block, upper)
 
 
 def solution(mesh):

time: 100 us -> 70.2 us (0.70)
  blocking collectives: 40.7 us -> 0 us
  Pallas kernels: 0 us -> 16.4 us
  other arithmetic: 11.8 us -> 5.14 us
  matrix products: 4.68 us -> 5.78 us
    psum x1 -> x0, blocking collectives: 40.7 us -> none  [on_device(): gram = lax.psum(partial_gram, ('gx', 'gy')) / float(entries)]
    pallas_call x0 -> x1, Pallas kernels: none -> 16.4 us  [factor_of(): pl.pallas_call(functools.partial(gram_kernel, nx, ny, entries), out_shape...]
    another operation x4 -> x0, other arithmetic: 6.03 us -> none  [the longest x3 3.59 us: on_device(): lower = jnp.linalg.cholesky(gram)]
    unnamed x16 -> x18, local copies, waits for them, and re-layouts: 6.64 us -> 6.57 us
  transfers between devices with their start and end apart: 8 -> 8, of which waited for: 4 -> 4; matrix products, arithmetic and copies ran while one was open for 13% -> 18% of each run, Pallas kernels for 0% -> 0%
where the time goes in v1:
time: 70.2 us; the launch traced here: 69.7 us
  local copies, waits for them, and re-layouts  17.5 us (25%)
  Pallas kernels  16.4 us (23%)
  starting transfers between devices  14 us (20%)
  waiting for transfers between devices  9.93 us (14%)
  matrix products  5.78 us (8%)
  other arithmetic  5.14 us (7%)
  between operations  0.9 us (1%)
    pallas_call x1, Pallas kernels, factor_of(): pl.pallas_call(functools.partial(gram_kernel, nx, ny, entries), out_shape...  16.4 us
    ppermute x4, starting transfers between devices, with_halo(): after = lax.ppermute(first, axis, down)  10 us
    unnamed x18, local copies, waits for them, and re-layouts  6.57 us
    ppermute x4, waiting for transfers between devices, with_halo(): before = lax.ppermute(last, axis, up)  6.43 us
    ppermute x4, starting transfers between devices, with_halo(): before = lax.ppermute(last, axis, up)  3.99 us
    slice x2, local copies, waits for them, and re-layouts, adjoint(): jnp.roll(inner, 1, axis=-1)  3.96 us
    slice x4, local copies, waits for them, and re-layouts, with_halo(): first = lax.slice_in_dim(value, 0, width, axis=dim)  3.94 us
    add x1, other arithmetic, adjoint(): return inner + ADVECT * (flux - coupling) + DIFFUSE * laplacian  3.88 us
  transfers between devices with their start and end apart: 8, of which 4 were waited for; matrix products, arithmetic and copies ran while one was open for 18% of the time, Pallas kernels for 0%

profile of v1, /device:TPU:0, one launch (start us, length us, event | category | flops | bytes accessed | tf_op | source)
XLA Modules:
  0.0 69.7 jit_solution(2478822953281161519)
XLA Ops:
  0.6 0.0 copy-start
  0.6 1.5 %fusion.32 = (f32[3,2,8,128]{3,2,1,0:T(8,128)}, f32[3,2,8,128]{3,2,1,0:T(8,128)}) fusion(f32[3,4,8,128]{3,2,1,0:T(8,128)} %param.2), kind=kLoop, calls=%fused_computation.67 | loop fusion | bytes 98304 | tf_op jit(solution)/shard_map/slice | solution.py:134
  2.1 4.5 %collective-permute-start.1 = (f32[3,2,8,128]{3,2,1,0:T(8,128)}, f32[3,2,8,128]{3,2,1,0:T(8,128)}, u32[]{:S(2)}, u32[]{:S(2)}) collective-permute-start(f32[3,2,8,128]{3,2,1,0:T(8,128)} %get-tuple-element.53), channel_id=1, source_target_pairs={{4,0},{8,4},{12,8},{16,12},{20,16},{24,20},{28,24},{0,28},{5,1},{9... | collective-permute-start | bytes 73736 | tf_op jit(solution)/shard_map/ppermute | solution.py:136
  6.7 0.0 collective-permute-start
  6.7 2.1 %fusion.22 = (f32[32,3,1,8,128]{4,3,2,0,1:T(8,128)}, f32[32,3,1,8,128]{4,3,2,0,1:T(8,128)}) fusion(f32[32,3,4,8,128]{4,3,2,1,0:T(8,128)} %param.3), kind=kLoop, calls=%fused_computation.57 | loop fusion | bytes 1572864 | tf_op jit(solution)/shard_map/slice | solution.py:134
  8.7 3.5 %collective-permute-start.4 = (f32[32,3,1,8,128]{4,3,2,0,1:T(8,128)}, f32[32,3,1,8,128]{4,3,2,0,1:T(8,128)S(1)}, u32[]{:S(2)}, u32[]{:S(2)}) collective-permute-start(f32[32,3,1,8,128]{4,3,2,0,1:T(8,128)} %get-tuple-element.21), channel_id=1, source_target_pairs={{4,0},{8,4},{12,8},{16,12},{20,16},{24,20},{28,24},{0,28},{5,1},{9... | collective-permute-start | bytes 1179656 | tf_op jit(solution)/shard_map/ppermute | solution.py:136
  12.3 0.0 collective-permute-start.5
  12.3 1.7 %fusion.23 = (f32[32,3,4,8,1]{4,3,2,0,1:T(8,128)S(1)}, f32[32,3,4,8,1]{4,3,2,0,1:T(8,128)}) fusion(f32[32,3,4,8,128]{4,3,2,1,0:T(8,128)S(1)} %copy-done), kind=kLoop, calls=%fused_computation.58 | loop fusion | bytes 3170304 | tf_op jit(solution)/shard_map/jit(_roll_static)/slice | solution.py:194
  14.0 2.2 %fusion.24 = (f32[32,3,4,8,127]{4,3,2,0,1:T(8,128)}, f32[32,3,4,8,127]{4,3,2,0,1:T(8,128)}) fusion(f32[32,3,4,8,128]{4,3,2,1,0:T(8,128)S(1)} %copy-done), kind=kLoop, calls=%fused_computation.59 | loop fusion | bytes 6266880 | tf_op jit(solution)/shard_map/jit(_roll_static)/slice | solution.py:194
  16.2 0.0 collective-permute-done
  16.2 0.7 %constant_dynamic-update-slice_fusion.2 = f32[3,8,8,128]{3,2,1,0:T(8,128)S(1)} fusion(f32[3,2,8,128]{3,2,1,0:T(8,128)} %collective-permute-done), kind=kLoop, calls=%fused_computation.44 | loop fusion | bytes 49152
  17.0 0.8 %constant_dynamic-update-slice_fusion.1 = f32[3,8,8,128]{3,2,1,0:T(8,128)S(1)} fusion(f32[3,8,8,128]{3,2,1,0:T(8,128)S(1)} %constant_dynamic-update-slice_fusion.2, f32[3,4,8,128]{3,2,1,0:T(8,128)} %param.2), kind=kLoop, calls=%fused_computation.43 | loop fusion | bytes 98304
  17.8 0.7 %constant_dynamic-update-slice_fusion = f32[3,8,8,128]{3,2,1,0:T(8,128)S(1)} fusion(f32[3,8,8,128]{3,2,1,0:T(8,128)S(1)} %constant_dynamic-update-slice_fusion.1, f32[3,2,8,128]{3,2,1,0:T(8,128)} %collective-permute-done.1), kind=kLoop, calls=%fused_computation.42 | loop fusion | bytes 49152 | tf_op jit(solution)/shard_map/concatenate | solution.py:137
  18.5 1.5 %collective-permute-start.2 = (f32[3,8,2,128]{3,2,1,0:T(2,128)S(1)}, f32[3,8,2,128]{3,2,1,0:T(2,128)S(1)}, u32[]{:S(2)}, u32[]{:S(2)}) collective-permute-start(f32[3,8,2,128]{3,2,1,0:T(2,128)S(1)} %get-tuple-element.51), channel_id=1, source_target_pairs={{0,1},{1,2},{2,3},{3,0},{4,5},{5,6},{6,7},{7,4},{8,9},{9,10},{10,1... | collective-permute-start | bytes 73736 | tf_op jit(solution)/shard_map/ppermute | solution.py:135
  20.1 1.4 %collective-permute-start.3 = (f32[3,8,2,128]{3,2,1,0:T(2,128)S(1)}, f32[3,8,2,128]{3,2,1,0:T(2,128)S(1)}, u32[]{:S(2)}, u32[]{:S(2)}) collective-permute-start(f32[3,8,2,128]{3,2,1,0:T(2,128)S(1)} %get-tuple-element.52), channel_id=1, source_target_pairs={{1,0},{2,1},{3,2},{0,3},{5,4},{6,5},{7,6},{4,7},{9,8},{10,9},{11,1... | collective-permute-start | bytes 73736 | tf_op jit(solution)/shard_map/ppermute | solution.py:136
  21.5 0.1 fusion.19
  21.6 0.1 copy.50
  21.7 1.6 %collective-permute-done.2 = f32[3,8,2,128]{3,2,1,0:T(2,128)S(1)} collective-permute-done((f32[3,8,2,128]{3,2,1,0:T(2,128)S(1)}, f32[3,8,2,128]{3,2,1,0:T(2,128)S(1)}, u32[]{:S(2)}, u32[]{:S(2)}) %collective-permute-start.2) | collective-permute-done | bytes 24608 | tf_op jit(solution)/shard_map/ppermute | solution.py:135
  23.3 0.6 collective-permute-done.3
  24.0 0.1 fusion.27
  24.1 0.1 fusion.28
  24.2 0.2 subtract_add_fusion
  24.4 0.1 fusion.29
  24.5 0.1 fusion.30
  24.6 0.1 slice_subtract_fusion
  24.7 0.5 multiply_reduce_fusion.2
  25.2 0.0 collective-permute-done.5
  25.2 1.0 %constant_dynamic-update-slice_fusion.5 = f32[32,3,6,8,128]{4,3,2,0,1:T(8,128)S(1)} fusion(f32[32,3,1,8,128]{4,3,2,0,1:T(8,128)} %collective-permute-done.5), kind=kLoop, calls=%fused_computation.47 | loop fusion | bytes 786432
  26.3 0.3 constant_dynamic-update-slice_fusion.4
  26.7 0.4 fusion.21
  27.1 2.4 %collective-permute-start.7 = (f32[32,3,6,1,128]{4,0,3,2,1:T(8,128)S(1)}, f32[32,3,6,1,128]{4,0,3,2,1:T(8,128)S(1)}, u32[]{:S(2)}, u32[]{:S(2)}) collective-permute-start(f32[32,3,6,1,128]{4,0,3,2,1:T(8,128)S(1)} %copy.47), channel_id=1, source_target_pairs={{0,1},{1,2},{2,3},{3,0},{4,5},{5,6},{6,7},{7,4},{8,9},{9,10},{10,1... | collective-permute-start | bytes 884744 | tf_op jit(solution)/shard_map/ppermute | solution.py:135
  29.5 0.5 collective-permute-start.6
  30.1 0.6 fusion.26
  30.6 0.0 copy-start.1
  30.7 0.6 fusion.25
  31.2 4.8 %collective-permute-done.7 = f32[32,3,6,1,128]{4,0,3,2,1:T(8,128)S(1)} collective-permute-done((f32[32,3,6,1,128]{4,0,3,2,1:T(8,128)S(1)}, f32[32,3,6,1,128]{4,0,3,2,1:T(8,128)S(1)}, u32[]{:S(2)}, u32[]{:S(2)}) %collective-permute-start.7) | collective-permute-done | bytes 294944 | tf_op jit(solution)/shard_map/ppermute | solution.py:135
  36.1 0.3 copy.48
  36.4 2.9 %collective-permute-done.6 = f32[32,3,6,1,128]{4,0,3,2,1:T(8,128)S(1)} collective-permute-done((f32[32,3,6,1,128]{4,0,3,2,1:T(8,128)S(1)}, f32[32,3,6,1,128]{4,0,3,2,1:T(8,128)S(1)}, u32[]{:S(2)}, u32[]{:S(2)}) %collective-permute-start.6) | collective-permute-done | bytes 294944 | tf_op jit(solution)/shard_map/ppermute | solution.py:136
  39.3 0.3 copy.46
  39.6 3.9 %fusion.4 = f32[32,3,4,8,128]{4,3,2,0,1:T(8,128)S(1)} fusion(f32[32,3,4,8,128]{4,3,2,0,1:T(8,128)S(1)} %copy.50, f32[32,3,4,8,1]{4,3,2,0,1:T(8,128)S(1)} %get-tuple-element.30, f32[32,3,4,8,127]{4,3,2,0,1:T(8,128)S(1)} %get-tuple-element.32, f32[32,3,4,8,127]{4,3,2,0,1:T(8,128)S(1)} %get-tuple-element.31, f32[32,3,4,8,1]{4,3,2,0,1:T(8,128)S(1)} %get-tuple-element.29, ...), kind=kLoop, calls=%fused_computation.10 | loop fusion | flops 12189696 | bytes 14811136 | tf_op jit(solution)/shard_map/add | solution.py:197
  43.5 2.8 %fusion.12.part = f32[32,32]{1,0:T(8,128)} fusion(f32[32,3,4,8,128]{4,3,2,0,1:T(8,128)S(1)} %fusion.4), kind=kOutput, calls=%fused_computation.22 | convolution fusion | flops 150994944 | bytes 1576960 | tf_op jit(solution)/shard_map/dot_general | solution.py:211
  46.3 0.1 copy.58
  46.4 0.9 %copy.80 = f32[4,8,96,128]{3,1,2,0:T(8,128)S(1)} copy(f32[4,8,96,128]{3,2,1,0:T(8,128)S(1)} %bitcast.42) | data formatting | bytes 3145728
  47.3 0.3 copy.64
  47.6 16.4 %shard_map.41 = (f32[32,32]{1,0:T(8,128)}, f32[32,32]{1,0:T(8,128)}) custom-call(f32[32,32]{1,0:T(8,128)} %fusion.12.part), custom_call_target="tpu_custom_call" | custom-call | tf_op jit(solution)/shard_map/pallas_call | solution.py:111
  64.0 3.0 %fusion.8 = f32[32,3,4,8,128]{4,0,3,2,1:T(8,128)S(1)} fusion(f32[3,4,8,128,32]{3,2,1,0,4:T(8,128)S(1)} %bitcast.41, f32[32,32]{1,0:T(8,128)} %get-tuple-element.4), kind=kOutput, calls=%fused_computation.15 | convolution fusion | flops 150994944 | bytes 3149824 | tf_op jit(solution)/shard_map/dot_general | solution.py:218
  67.0 2.1 %copy.60 = f32[32,3,4,8,128]{4,3,2,1,0:T(8,128)} copy(f32[32,3,4,8,128]{4,0,3,2,1:T(8,128)S(1)} %fusion.8) | data formatting | bytes 3145728
  69.1 0.6 copy.86
  (18 shorter events, 0.2 us)
Async XLA Ops:
  0.6 11.6 %copy-start = (f32[32,3,4,8,128]{4,3,2,1,0:T(8,128)S(1)}, f32[32,3,4,8,128]{4,3,2,1,0:T(8,128)}, u32[]{:S(2)}) copy-start(f32[32,3,4,8,128]{4,3,2,1,0:T(8,128)} %param.3) | copy-start | bytes 4718596
  2.1 15.6 %collective-permute-start.1 = (f32[3,2,8,128]{3,2,1,0:T(8,128)}, f32[3,2,8,128]{3,2,1,0:T(8,128)}, u32[]{:S(2)}, u32[]{:S(2)}) collective-permute-start(f32[3,2,8,128]{3,2,1,0:T(8,128)} %get-tuple-element.53), channel_id=1, source_target_pairs={{4,0},{8,4},{12,8},{16,12},{20,16},{24,20},{28,24},{0,28},{5,1},{9... | collective-permute-start | bytes 73736 | tf_op jit(solution)/shard_map/ppermute | solution.py:136
  6.7 9.6 %collective-permute-start = (f32[3,2,8,128]{3,2,1,0:T(8,128)}, f32[3,2,8,128]{3,2,1,0:T(8,128)}, u32[]{:S(2)}, u32[]{:S(2)}) collective-permute-start(f32[3,2,8,128]{3,2,1,0:T(8,128)} %get-tuple-element.54), channel_id=1, source_target_pairs={{0,4},{4,8},{8,12},{12,16},{16,20},{20,24},{24,28},{28,0},{1,5},{5... | collective-permute-start | bytes 73736 | tf_op jit(solution)/shard_map/ppermute | solution.py:135
  8.7 17.9 %collective-permute-start.4 = (f32[32,3,1,8,128]{4,3,2,0,1:T(8,128)}, f32[32,3,1,8,128]{4,3,2,0,1:T(8,128)S(1)}, u32[]{:S(2)}, u32[]{:S(2)}) collective-permute-start(f32[32,3,1,8,128]{4,3,2,0,1:T(8,128)} %get-tuple-element.21), channel_id=1, source_target_pairs={{4,0},{8,4},{12,8},{16,12},{20,16},{24,20},{28,24},{0,28},{5,1},{9... | collective-permute-start | bytes 1179656 | tf_op jit(solution)/shard_map/ppermute | solution.py:136
  12.3 13.0 %collective-permute-start.5 = (f32[32,3,1,8,128]{4,3,2,0,1:T(8,128)}, f32[32,3,1,8,128]{4,3,2,0,1:T(8,128)}, u32[]{:S(2)}, u32[]{:S(2)}) collective-permute-start(f32[32,3,1,8,128]{4,3,2,0,1:T(8,128)} %get-tuple-element.22), channel_id=1, source_target_pairs={{0,4},{4,8},{8,12},{12,16},{16,20},{20,24},{24,28},{28,0},{1,5},{5... | collective-permute-start | bytes 1179656 | tf_op jit(solution)/shard_map/ppermute | solution.py:135
  18.5 4.8 %collective-permute-start.2 = (f32[3,8,2,128]{3,2,1,0:T(2,128)S(1)}, f32[3,8,2,128]{3,2,1,0:T(2,128)S(1)}, u32[]{:S(2)}, u32[]{:S(2)}) collective-permute-start(f32[3,8,2,128]{3,2,1,0:T(2,128)S(1)} %get-tuple-element.51), channel_id=1, source_target_pairs={{0,1},{1,2},{2,3},{3,0},{4,5},{5,6},{6,7},{7,4},{8,9},{9,10},{10,1... | collective-permute-start | bytes 73736 | tf_op jit(solution)/shard_map/ppermute | solution.py:135
  20.1 3.8 %collective-permute-start.3 = (f32[3,8,2,128]{3,2,1,0:T(2,128)S(1)}, f32[3,8,2,128]{3,2,1,0:T(2,128)S(1)}, u32[]{:S(2)}, u32[]{:S(2)}) collective-permute-start(f32[3,8,2,128]{3,2,1,0:T(2,128)S(1)} %get-tuple-element.52), channel_id=1, source_target_pairs={{1,0},{2,1},{3,2},{0,3},{5,4},{6,5},{7,6},{4,7},{9,8},{10,9},{11,1... | collective-permute-start | bytes 73736 | tf_op jit(solution)/shard_map/ppermute | solution.py:136
  27.1 9.0 %collective-permute-start.7 = (f32[32,3,6,1,128]{4,0,3,2,1:T(8,128)S(1)}, f32[32,3,6,1,128]{4,0,3,2,1:T(8,128)S(1)}, u32[]{:S(2)}, u32[]{:S(2)}) collective-permute-start(f32[32,3,6,1,128]{4,0,3,2,1:T(8,128)S(1)} %copy.47), channel_id=1, source_target_pairs={{0,1},{1,2},{2,3},{3,0},{4,5},{5,6},{6,7},{7,4},{8,9},{9,10},{10,1... | collective-permute-start | bytes 884744 | tf_op jit(solution)/shard_map/ppermute | solution.py:135
  29.5 9.7 %collective-permute-start.6 = (f32[32,3,6,1,128]{4,0,3,2,1:T(8,128)S(1)}, f32[32,3,6,1,128]{4,0,3,2,1:T(8,128)S(1)}, u32[]{:S(2)}, u32[]{:S(2)}) collective-permute-start(f32[32,3,6,1,128]{4,0,3,2,1:T(8,128)S(1)} %copy.45), channel_id=1, source_target_pairs={{1,0},{2,1},{3,2},{0,3},{5,4},{6,5},{7,6},{4,7},{9,8},{10,9},{11,1... | collective-permute-start | bytes 884744 | tf_op jit(solution)/shard_map/ppermute | solution.py:136
  30.6 8.9 %copy-start.1 = (f32[32,3,4,8,1]{4,3,2,0,1:T(8,128)S(1)}, f32[32,3,4,8,1]{4,3,2,0,1:T(8,128)}, u32[]{:S(2)}) copy-start(f32[32,3,4,8,1]{4,3,2,0,1:T(8,128)} %get-tuple-element.26) | copy-start | bytes 36868
  30.7 8.9 %copy-start.2 = (f32[32,3,4,8,127]{4,3,2,0,1:T(8,128)S(1)}, f32[32,3,4,8,127]{4,3,2,0,1:T(8,128)}, u32[]{:S(2)}) copy-start(f32[32,3,4,8,127]{4,3,2,0,1:T(8,128)} %get-tuple-element.27) | copy-start | bytes 4681732
  30.7 8.9 %copy-start.3 = (f32[32,3,4,8,127]{4,3,2,0,1:T(8,128)S(1)}, f32[32,3,4,8,127]{4,3,2,0,1:T(8,128)}, u32[]{:S(2)}) copy-start(f32[32,3,4,8,127]{4,3,2,0,1:T(8,128)} %get-tuple-element.28) | copy-start | bytes 4681732
  67.0 2.1 %copy-start.4 = (f32[32,32]{1,0:T(8,128)S(1)}, f32[32,32]{1,0:T(8,128)}, u32[]{:S(2)}) copy-start(f32[32,32]{1,0:T(8,128)} %get-tuple-element.59) | copy-start | bytes 12292

commit v2 on v1

v2 whole, which is shorter than its diff:
```python
import functools
import math

import jax
import jax.numpy as jnp
from jax import lax
from jax.experimental import pallas as pl
from jax.experimental.pallas import tpu as pltpu
from jax.sharding import PartitionSpec as P

ADVECT = 0.1
DIFFUSE = 0.08
DRIVE_SCALE = 0.25
WAVENUMBER = 4.0
MESH = pl.DeviceIdType.MESH


def positions(nx, ny):
    gx, gy = lax.axis_index("gx"), lax.axis_index("gy")
    return (gx, gy, lax.rem(gx, 2) * ny + gy, gx // 2)


def plane_peer(nx, ny, step):
    gx, gy, mine, line = positions(nx, ny)
    place = lax.rem(mine + step, 2 * ny)
    return (line * 2 + place // ny, lax.rem(place, ny))


def line_peer(nx, ny, step):
    gx, gy, mine, line = positions(nx, ny)
    return (lax.rem(line + step, nx // 2) * 2 + lax.rem(gx, 2), gy)


def total_gram(nx, ny, plane, line, send_a, recv_a, send_b, recv_b):
    gx, gy, mine, place = positions(nx, ny)
    members, planes = 2 * ny, nx // 2

    def hop_a(step):
        return pltpu.make_async_remote_copy(
            plane.at[mine], plane.at[mine], send_a.at[step], recv_a.at[step],
            device_id=plane_peer(nx, ny, step), device_id_type=MESH)

    def hop_b(step):
        return pltpu.make_async_remote_copy(
            line.at[place], line.at[place], send_b.at[step], recv_b.at[step],
            device_id=line_peer(nx, ny, step), device_id_type=MESH)

    for step in range(1, members):
        hop_a(step).start()
    for step in range(1, members):
        hop_a(step).wait_recv()
    total = plane[0]
    for i in range(1, members):
        total = total + plane[i]
    line[place] = total
    for step in range(1, planes):
        hop_b(step).start()
    for step in range(1, planes):
        hop_b(step).wait_recv()
    total = line[0]
    for i in range(1, planes):
        total = total + line[i]
    for step in range(1, members):
        hop_a(step).wait_send()
    for step in range(1, planes):
        hop_b(step).wait_send()
    return total


def eliminate(gram):
    size = gram.shape[0]
    rows = lax.broadcasted_iota(jnp.int32, (size, size), 0)
    cols = lax.broadcasted_iota(jnp.int32, (size, size), 1)
    left, right = gram, (rows == cols).astype(jnp.float32)
    row = lax.broadcasted_iota(jnp.int32, (size, 1), 0)
    m = jnp.concatenate([left, right], axis=1)
    pivots = jnp.zeros((size, 1), jnp.float32)
    for k in range(size):
        pivot_row = m[k : k + 1, :]
        pivot = pivot_row[:, k : k + 1]
        column = m[:, k : k + 1]
        pivots = jnp.where(row == k, pivot, pivots)
        factor = jnp.where(row > k, column / pivot, 0.0)
        m = m - factor * pivot_row
    m = m * lax.rsqrt(pivots)
    upper = jnp.where(cols >= rows, m[:, :size], 0.0)
    return upper, m[:, size:]


WIDE = 2


def neighbour(nx, ny, dx, dy):
    return (lax.rem(lax.axis_index("gx") + dx + nx, nx), lax.rem(lax.axis_index("gy") + dy + ny, ny))


SIDES = ((-1, 0), (1, 0), (0, -1), (0, 1), (-1, -1), (-1, 1), (1, -1), (1, 1))


def meet(nx, ny):
    barrier = pltpu.get_barrier_semaphore()
    peers = [neighbour(nx, ny, dx, dy) for dx, dy in SIDES if dx]
    peers += [plane_peer(nx, ny, step) for step in range(1, 2 * ny)]
    peers += [line_peer(nx, ny, step) for step in range(1, nx // 2)]
    for peer in peers:
        pl.semaphore_signal(barrier, inc=1, device_id=peer, device_id_type=MESH)
    return barrier, len(peers)


def advance_rows(bext, forcing, x, wide_y):
    rows = wide_y + 2
    centre = [bext[c, x + 1, 1 : 1 + rows, :] for c in range(3)]
    advanced = []
    for c in range(3):
        east, west = bext[c, x + 2, 1 : 1 + rows, :], bext[c, x, 1 : 1 + rows, :]
        north, south = bext[c, x + 1, 2 : 2 + rows, :], bext[c, x + 1, 0:rows, :]
        up, down = pltpu.roll(centre[c], 127, axis=1), pltpu.roll(centre[c], 1, axis=1)
        laplacian = east + west + north + south + up + down - 6.0 * centre[c]
        advection = centre[0] * (east - west) + centre[1] * (north - south) + centre[2] * (up - down)
        value = centre[c] + DIFFUSE * laplacian - ADVECT * advection
        advanced.append(value + forcing if c == 0 else value)
    return advanced


def step_kernel(
    nx, ny, entries, base, a2, q2, upper, edges, bx, by, bc, bext, adv, coef, at, split, gram_acc,
    plane, line, base_send, base_recv, halo_send, halo_recv, send_a, recv_a, send_b, recv_b,
):
    wide_x, wide_y = base.shape[1], base.shape[2]
    vectors = at.shape[3]
    stride = 3 * wide_x * wide_y
    gx, gy, mine, place = positions(nx, ny)
    barrier, met = meet(nx, ny)

    for side, start in ((0, 0), (1, wide_y - WIDE)):
        for c in range(3):
            edges[side, :, c] = base[c, :, start : start + WIDE, :]

    def move(c):
        def plane_of(x, carry):
            for y in range(wide_y):
                at[c, x + 1, y + 1] = a2[pl.ds((c * wide_x + x) * wide_y + y, vectors, stride=stride), :]
            return carry
        lax.fori_loop(0, wide_x, plane_of, 0)

    def base_copy(i):
        dx, dy = SIDES[i]
        near_x = pl.ds(0, WIDE) if dx < 0 else pl.ds(wide_x - WIDE, WIDE)
        side = 0 if dy < 0 else 1
        if dy == 0:
            src, dst = base.at[:, near_x], bx.at[(1 - dx) // 2]
        elif dx == 0:
            src, dst = edges.at[side], by.at[1 - side]
        else:
            src, dst = edges.at[side, near_x], bc.at[(1 - dx) // 2, 1 - side]
        return pltpu.make_async_remote_copy(
            src, dst, base_send.at[i], base_recv.at[i],
            device_id=neighbour(nx, ny, dx, dy), device_id_type=MESH)

    def halo_copy(c, i):
        dx, dy = SIDES[i]
        inner_x, inner_y = pl.ds(1, wide_x), pl.ds(1, wide_y)
        if dx < 0:
            src, dst = at.at[c, 1, inner_y], at.at[c, wide_x + 1, inner_y]
        elif dx > 0:
            src, dst = at.at[c, wide_x, inner_y], at.at[c, 0, inner_y]
        elif dy < 0:
            src, dst = at.at[c, inner_x, 1], at.at[c, inner_x, wide_y + 1]
        else:
            src, dst = at.at[c, inner_x, wide_y], at.at[c, inner_x, 0]
        return pltpu.make_async_remote_copy(
            src, dst, halo_send.at[c, i], halo_recv.at[c, i],
            device_id=neighbour(nx, ny, dx, dy), device_id_type=MESH)

    move(0)
    pl.semaphore_wait(barrier, met)
    for i in range(8):
        base_copy(i).start()
    for c in range(3):
        for i in range(4):
            halo_copy(c, i).start()
        if c < 2:
            move(c + 1)

    for c in range(3):
        bext[c, WIDE : WIDE + wide_x, WIDE : WIDE + wide_y, :] = base[c]
    for i in range(8):
        base_copy(i).wait_recv()
    low, high = WIDE + wide_x, WIDE + wide_y
    for c in range(3):
        for sx, start_x in ((0, 0), (1, low)):
            bext[c, start_x : start_x + WIDE, WIDE:high, :] = bx[sx, c]
            for sy, start_y in ((0, 0), (1, high)):
                bext[c, start_x : start_x + WIDE, start_y : start_y + WIDE, :] = bc[sx, sy, :, c]
        for sy, start_y in ((0, 0), (1, high)):
            bext[c, WIDE:low, start_y : start_y + WIDE, :] = by[sy, :, c]

    ny_total = wide_y * ny
    column = lax.broadcasted_iota(jnp.int32, (wide_y + 2, 128), 0) + (gy * wide_y + ny_total - 1)
    phases = 2.0 * math.pi * WAVENUMBER * lax.rem(column, ny_total).astype(jnp.float32) / float(ny_total)
    forcing = DRIVE_SCALE * jnp.sin(phases)
    for x in range(wide_x + 2):
        for c, value in enumerate(advance_rows(bext, forcing, x, wide_y)):
            adv[c, x, 0 : wide_y + 2, :] = value
    for x in range(wide_x):
        inner = [adv[m, x + 1, 1 : 1 + wide_y, :] for m in range(3)]
        coef[0, x] = ADVECT * adv[0, x + 2, 1 : 1 + wide_y, :] + DIFFUSE
        coef[1, x] = DIFFUSE - ADVECT * adv[0, x, 1 : 1 + wide_y, :]
        coef[2, x] = ADVECT * adv[1, x + 1, 2 : 2 + wide_y, :] + DIFFUSE
        coef[3, x] = DIFFUSE - ADVECT * adv[1, x + 1, 0:wide_y, :]
        coef[4, x] = ADVECT * inner[2] + DIFFUSE
        coef[5, x] = DIFFUSE - ADVECT * inner[2]
        for m in range(3):
            slopes = (
                adv[m, x + 2, 1 : 1 + wide_y, :] - adv[m, x, 1 : 1 + wide_y, :],
                adv[m, x + 1, 2 : 2 + wide_y, :] - adv[m, x + 1, 0:wide_y, :],
                pltpu.roll(inner[m], 127, axis=1) - pltpu.roll(inner[m], 1, axis=1),
            )
            for i in range(3):
                own = 1.0 - 6.0 * DIFFUSE if i == m else 0.0
                coef[6 + 3 * i + m, x] = own - ADVECT * slopes[i]

    gram_acc[...] = jnp.zeros_like(gram_acc)
    for c in range(3):
        for i in range(4):
            halo_copy(c, i).wait_recv()

        def plane_of(x, carry, c=c):
            columns = []
            for y in range(wide_y):
                k = [coef[n, x, y : y + 1, :] for n in range(6)]
                k += [coef[6 + 3 * c + m, x, y : y + 1, :] for m in range(3)]
                own = [at[m, x + 1, y + 1] for m in range(3)]
                value = k[0] * at[c, x + 2, y + 1] + k[1] * at[c, x, y + 1]
                value += k[2] * at[c, x + 1, y + 2] + k[3] * at[c, x + 1, y]
                value += pltpu.roll(k[4] * own[c], 127, axis=1) + pltpu.roll(k[5] * own[c], 1, axis=1)
                value += k[6] * own[0] + k[7] * own[1] + k[8] * own[2]
                columns.append(value)
            updated = jnp.concatenate(columns, axis=1)
            first = updated.astype(jnp.bfloat16)
            second = (updated - first.astype(jnp.float32)).astype(jnp.bfloat16)
            both = jnp.concatenate([first, second], axis=0)
            split[c * wide_x + x] = both
            gram_acc[...] += lax.dot_general(
                both, both, (((1,), (1,)), ((), ())), preferred_element_type=jnp.float32)
            return carry

        lax.fori_loop(0, wide_x, plane_of, 0)

    g = gram_acc[...]
    g = g[:vectors] + g[vectors:]
    plane[mine] = g[:, :vectors] + g[:, vectors:]
    gram = total_gram(nx, ny, plane, line, send_a, recv_a, send_b, recv_b) / entries
    upper[...], inverse = eliminate(gram)
    first = inverse.astype(jnp.bfloat16)
    second = (inverse - first.astype(jnp.float32)).astype(jnp.bfloat16)
    weights = jnp.concatenate([first, first, second, second], axis=1)

    def out_group(n, carry):
        both = split[n]
        q = jnp.dot(weights, jnp.concatenate([both, both], axis=0), preferred_element_type=jnp.float32)
        for y in range(wide_y):
            q2[pl.ds(n * wide_y + y, vectors, stride=stride), :] = q[:, y * 128 : (y + 1) * 128]
        return carry

    lax.fori_loop(0, 3 * wide_x, out_group, 0)
    for i in range(8):
        base_copy(i).wait_send()
    for c in range(3):
        for i in range(4):
            halo_copy(c, i).wait_send()


def on_device(base_state, adjoint_block):
    nx, ny = lax.axis_size("gx"), lax.axis_size("gy")
    vectors, _, wide_x, wide_y, lanes = adjoint_block.shape
    assert lanes == 128
    entries = float(3 * wide_x * wide_y * lanes * nx * ny)
    f32, dma = jnp.float32, pltpu.SemaphoreType.DMA
    vmem = pl.BlockSpec(memory_space=pltpu.VMEM)
    rows = vectors * 3 * wide_x * wide_y
    q, upper = pl.pallas_call(
        functools.partial(step_kernel, nx, ny, entries),
        out_shape=(jax.ShapeDtypeStruct((rows, 128), f32), jax.ShapeDtypeStruct((vectors, vectors), f32)),
        in_specs=[vmem, vmem],
        out_specs=(vmem, vmem),
        scratch_shapes=[
            pltpu.VMEM((2, wide_x, 3, WIDE, 128), f32),
            pltpu.VMEM((2, 3, WIDE, wide_y, 128), f32),
            pltpu.VMEM((2, wide_x, 3, WIDE, 128), f32),
            pltpu.VMEM((2, 2, WIDE, 3, WIDE, 128), f32),
            pltpu.VMEM((3, wide_x + 4, wide_y + 8, 128), f32),
            pltpu.VMEM((3, wide_x + 2, wide_y + 8, 128), f32),
            pltpu.VMEM((15, wide_x, wide_y, 128), f32),
            pltpu.VMEM((3, wide_x + 2, wide_y + 2, vectors, 128), f32),
            pltpu.VMEM((3 * wide_x, 2 * vectors, wide_y * 128), jnp.bfloat16),
            pltpu.VMEM((2 * vectors, 2 * vectors), f32),
            pltpu.VMEM((2 * ny, vectors, vectors), f32),
            pltpu.VMEM((nx // 2, vectors, vectors), f32),
            dma((8,)), dma((8,)), dma((3, 4)), dma((3, 4)),
            dma((2 * ny,)), dma((2 * ny,)), dma((nx // 2,)), dma((nx // 2,)),
        ],
        compiler_params=pltpu.CompilerParams(collective_id=0, has_side_effects=True),
    )(base_state, adjoint_block.reshape(rows, 128))
    return (q.reshape(adjoint_block.shape), upper)


def solution(mesh):
    in_specs = (P(None, "gx", "gy", None), P(None, None, "gx", "gy", None))
    out_specs = (P(None, None, "gx", "gy", None), P())
    return jax.shard_map(
        on_device, mesh=mesh, in_specs=in_specs, out_specs=out_specs, check_vma=False
    )
```

time: 70.2 us -> 38.4 us (0.55)
  Pallas kernels: 16.4 us -> 34.3 us
  local copies, waits for them, and re-layouts: 17.5 us -> 3.29 us
  starting transfers between devices: 14 us -> 0 us
  waiting for transfers between devices: 9.93 us -> 0 us
  matrix products: 5.78 us -> 0 us
  other arithmetic: 5.14 us -> 0 us
    pallas_call x1, Pallas kernels: 16.4 us -> 34.3 us  [on_device(): pl.pallas_call(functools.partial(step_kernel, nx, ny, entries), out_shape...]
    ppermute x8 -> x0, starting transfers between devices: 14 us -> none  [the longest x4 10 us: with_halo(): after = lax.ppermute(first, axis, down)]
    ppermute x8 -> x0, waiting for transfers between devices: 9.93 us -> none  [the longest x4 6.43 us: with_halo(): before = lax.ppermute(last, axis, up)]
    slice x14 -> x0, local copies, waits for them, and re-layouts: 9.44 us -> none  [the longest x2 3.96 us: adjoint(): jnp.roll(inner, 1, axis=-1)]
    dot_general x2 -> x0, matrix products: 5.78 us -> none  [the longest x1 3 us: on_device(): jnp.dot(inverse, flat, precision=lax.Precision.HIGHEST, preferred_element...]
    add x2 -> x0, other arithmetic: 4.08 us -> none  [the longest x1 3.88 us: adjoint(): return inner + ADVECT * (flux - coupling) + DIFFUSE * laplacian]
    unnamed x18 -> x4, local copies, waits for them, and re-layouts: 6.57 us -> 3.29 us
    concatenate x2 -> x0, local copies, waits for them, and re-layouts: 0.77 us -> none  [with_halo(): value = jnp.concatenate([before, value, after], axis=dim)]
  transfers between devices with their start and end apart: 8 -> 0, of which waited for: 4 -> 0; matrix products, arithmetic and copies ran while one was open for 18% -> 0% of each run, Pallas kernels for 0% -> 0%
where the time goes in v2:
time: 38.4 us; the launch traced here: 38.3 us
  Pallas kernels  34.3 us (89%)
  local copies, waits for them, and re-layouts  3.29 us (9%)
  between operations  0.65 us (2%)
    pallas_call x1, Pallas kernels, on_device(): pl.pallas_call(functools.partial(step_kernel, nx, ny, entries), out_shape...  34.3 us
    unnamed x4, local copies, waits for them, and re-layouts  3.29 us

profile of v2, /device:TPU:0, one launch (start us, length us, event | category | flops | bytes accessed | tf_op | source)
XLA Modules:
  0.0 38.3 jit_solution(3538032750091824047)
XLA Ops:
  0.6 34.3 %shard_map.41 = (f32[3072,128]{1,0:T(8,128)}, f32[32,32]{1,0:T(8,128)}) custom-call(f32[3,4,8,128]{3,2,1,0:T(8,128)} %base.1, f32[3072,128]{1,0:T(8,128)} %bitcast.2), custom_call_target="tpu_custom_call" | custom-call | tf_op jit(solution)/shard_map/pallas_call | solution.py:282
  35.0 0.0 copy-start
  35.0 2.7 %copy.6 = f32[32,3,4,8,128]{4,3,2,1,0:T(8,128)} copy(f32[32,3,4,8,128]{4,3,2,1,0:T(8,128)} %bitcast.3) | data formatting | bytes 3145728
  37.7 0.0 copy-done
  37.7 0.6 %copy.7 = f32[32,32]{1,0:T(8,128)} copy(f32[32,32]{1,0:T(8,128)S(1)} %copy-done) | data formatting | bytes 8192
Async XLA Ops:
  35.0 2.7 %copy-start = (f32[32,32]{1,0:T(8,128)S(1)}, f32[32,32]{1,0:T(8,128)}, u32[]{:S(2)}) copy-start(f32[32,32]{1,0:T(8,128)} %get-tuple-element.9) | copy-start | bytes 12292

commit v3 on v2

--- a/solution.py
+++ b/solution.py
@@ -123,14 +123,19 @@
 
 
 def step_kernel(
-    nx, ny, entries, base, a2, q2, upper, edges, bx, by, bc, bext, adv, coef, at, split, gram_acc,
-    plane, line, base_send, base_recv, halo_send, halo_recv, send_a, recv_a, send_b, recv_b,
+    nx, ny, entries, base_in, a_in, pieces, gram, base, a2, in_sem, edges, bx, by, bc, bext, adv, coef, at, split, gram_acc,
+    plane, line, base_send, base_recv, halo_send, halo_recv, send_a, recv_a, send_b, recv_b, out_sem,
 ):
     wide_x, wide_y = base.shape[1], base.shape[2]
     vectors = at.shape[3]
     stride = 3 * wide_x * wide_y
     gx, gy, mine, place = positions(nx, ny)
     barrier, met = meet(nx, ny)
+    base_load = pltpu.make_async_copy(base_in, base, in_sem.at[0])
+    load = pltpu.make_async_copy(a_in, a2, in_sem.at[1])
+    base_load.start()
+    load.start()
+    base_load.wait()
 
     for side, start in ((0, 0), (1, wide_y - WIDE)):
         for c in range(3):
@@ -172,10 +177,11 @@
             src, dst, halo_send.at[c, i], halo_recv.at[c, i],
             device_id=neighbour(nx, ny, dx, dy), device_id_type=MESH)
 
-    move(0)
     pl.semaphore_wait(barrier, met)
     for i in range(8):
         base_copy(i).start()
+    load.wait()
+    move(0)
     for c in range(3):
         for i in range(4):
             halo_copy(c, i).start()
@@ -220,6 +226,10 @@
                 own = 1.0 - 6.0 * DIFFUSE if i == m else 0.0
                 coef[6 + 3 * i + m, x] = own - ADVECT * slopes[i]
 
+    def out_copy(c):
+        part = pl.ds(c * wide_x, wide_x)
+        return pltpu.make_async_copy(split.at[part], pieces.at[part], out_sem.at[c])
+
     gram_acc[...] = jnp.zeros_like(gram_acc)
     for c in range(3):
         for i in range(4):
@@ -246,29 +256,55 @@
             return carry
 
         lax.fori_loop(0, wide_x, plane_of, 0)
+        if c:
+            out_copy(c - 1).start()
 
     g = gram_acc[...]
     g = g[:vectors] + g[vectors:]
     plane[mine] = g[:, :vectors] + g[:, vectors:]
-    gram = total_gram(nx, ny, plane, line, send_a, recv_a, send_b, recv_b) / entries
-    upper[...], inverse = eliminate(gram)
+    out_copy(2).start()
+    gram[...] = total_gram(nx, ny, plane, line, send_a, recv_a, send_b, recv_b) / entries
+    for c in range(3):
+        out_copy(c).wait()
+    for i in range(8):
+        base_copy(i).wait_send()
+    for c in range(3):
+        for i in range(4):
+            halo_copy(c, i).wait_send()
+
+
+def factor_kernel(gram, pieces, q, upper, split, result, in_sem, out_sem):
+    groups, vectors, wide_y = q.shape[1], q.shape[0], q.shape[2]
+
+    def load(n):
+        return pltpu.make_async_copy(pieces.at[n], split.at[n], in_sem.at[n])
+
+    def store(n):
+        return pltpu.make_async_copy(result.at[:, n], q.at[:, n], out_sem.at[n])
+
+    def over(body):
+        def run(n, carry):
+            body(n)
+            return carry
+        lax.fori_loop(0, groups, run, 0)
+
+    over(lambda n: load(n).start())
+    upper[...], inverse = eliminate(gram[...])
     first = inverse.astype(jnp.bfloat16)
     second = (inverse - first.astype(jnp.float32)).astype(jnp.bfloat16)
     weights = jnp.concatenate([first, first, second, second], axis=1)
-
-    def out_group(n, carry):
+    flat = result.reshape(vectors * groups * wide_y, 128)
+
+    def group(n):
+        load(n).wait()
         both = split[n]
-        q = jnp.dot(weights, jnp.concatenate([both, both], axis=0), preferred_element_type=jnp.float32)
+        value = jnp.dot(weights, jnp.concatenate([both, both], axis=0), preferred_element_type=jnp.float32)
         for y in range(wide_y):
-            q2[pl.ds(n * wide_y + y, vectors, stride=stride), :] = q[:, y * 128 : (y + 1) * 128]
-        return carry
-
-    lax.fori_loop(0, 3 * wide_x, out_group, 0)
-    for i in range(8):
-        base_copy(i).wait_send()
-    for c in range(3):
-        for i in range(4):
-            halo_copy(c, i).wait_send()
+            flat[pl.ds(n * wide_y + y, vectors, stride=groups * wide_y), :] = value[:, y * 128 : (y + 1) * 128]
+        store(n).start()
+
+    over(group)
+    over(lambda n: store(n).wait())
 
 
 def on_device(base_state, adjoint_block):
@@ -279,12 +315,17 @@
     f32, dma = jnp.float32, pltpu.SemaphoreType.DMA
     vmem = pl.BlockSpec(memory_space=pltpu.VMEM)
     rows = vectors * 3 * wide_x * wide_y
-    q, upper = pl.pallas_call(
+    split_shape = (3 * wide_x, 2 * vectors, wide_y * 128)
+    any_space = pl.BlockSpec(memory_space=pl.ANY)
+    pieces, gram = pl.pallas_call(
         functools.partial(step_kernel, nx, ny, entries),
-        out_shape=(jax.ShapeDtypeStruct((rows, 128), f32), jax.ShapeDtypeStruct((vectors, vectors), f32)),
-        in_specs=[vmem, vmem],
-        out_specs=(vmem, vmem),
+        out_shape=(jax.ShapeDtypeStruct(split_shape, jnp.bfloat16), jax.ShapeDtypeStruct((vectors, vectors), f32)),
+        in_specs=[any_space, any_space],
+        out_specs=(any_space, vmem),
         scratch_shapes=[
+            pltpu.VMEM(base_state.shape, f32),
+            pltpu.VMEM((rows, 128), f32),
+            dma((2,)),
             pltpu.VMEM((2, wide_x, 3, WIDE, 128), f32),
             pltpu.VMEM((2, 3, WIDE, wide_y, 128), f32),
             pltpu.VMEM((2, wide_x, 3, WIDE, 128), f32),
@@ -293,15 +334,27 @@
             pltpu.VMEM((3, wide_x + 2, wide_y + 8, 128), f32),
             pltpu.VMEM((15, wide_x, wide_y, 128), f32),
             pltpu.VMEM((3, wide_x + 2, wide_y + 2, vectors, 128), f32),
-            pltpu.VMEM((3 * wide_x, 2 * vectors, wide_y * 128), jnp.bfloat16),
+            pltpu.VMEM(split_shape, jnp.bfloat16),
             pltpu.VMEM((2 * vectors, 2 * vectors), f32),
             pltpu.VMEM((2 * ny, vectors, vectors), f32),
             pltpu.VMEM((nx // 2, vectors, vectors), f32),
             dma((8,)), dma((8,)), dma((3, 4)), dma((3, 4)),
-            dma((2 * ny,)), dma((2 * ny,)), dma((nx // 2,)), dma((nx // 2,)),
+            dma((2 * ny,)), dma((2 * ny,)), dma((nx // 2,)), dma((nx // 2,)), dma((3,)),
         ],
         compiler_params=pltpu.CompilerParams(collective_id=0, has_side_effects=True),
     )(base_state, adjoint_block.reshape(rows, 128))
+    q_shape = (vectors, 3 * wide_x, wide_y, 128)
+    q, upper = pl.pallas_call(
+        factor_kernel,
+        out_shape=(jax.ShapeDtypeStruct(q_shape, f32), jax.ShapeDtypeStruct((vectors, vectors), f32)),
+        in_specs=[vmem, any_space],
+        out_specs=(any_space, vmem),
+        scratch_shapes=[
+            pltpu.VMEM(split_shape, jnp.bfloat16),
+            pltpu.VMEM(q_shape, f32),
+            dma((3 * wide_x,)), dma((3 * wide_x,)),
+        ],
+    )(gram, pieces)
     return (q.reshape(adjoint_block.shape), upper)
 
 

time: 38.4 us -> 35.6 us (0.927)
  local copies, waits for them, and re-layouts: 3.29 us -> 0 us
  Pallas kernels: 34.3 us -> 34.7 us
    pallas_call x0 -> x1, Pallas kernels: none -> 7.66 us  [on_device(): pl.pallas_call(factor_kernel, out_shape=(jax.ShapeDtypeStruct(q_shape, f3...]
    pallas_call x1, Pallas kernels: 34.3 us -> 27.1 us  [on_device(): pl.pallas_call(functools.partial(step_kernel, nx, ny, entries), out_shape...]
    unnamed x4 -> x0, local copies, waits for them, and re-layouts: 3.29 us -> none
where the time goes in v3:
time: 35.6 us; the launch traced here: 35.3 us
  Pallas kernels  34.7 us (97%)
  between operations  0.64 us (2%)
    pallas_call x1, Pallas kernels, on_device(): pl.pallas_call(functools.partial(step_kernel, nx, ny, entries), out_shape...  27.1 us
    pallas_call x1, Pallas kernels, on_device(): pl.pallas_call(factor_kernel, out_shape=(jax.ShapeDtypeStruct(q_shape, f3...  7.66 us

profile of v3, /device:TPU:0, one launch (start us, length us, event | category | flops | bytes accessed | tf_op | source)
XLA Modules:
  0.0 35.3 jit_solution(12739244913718409130)
XLA Ops:
  0.6 27.1 %shard_map.41 = (bf16[12,64,1024]{2,1,0:T(8,128)(2,1)}, f32[32,32]{1,0:T(8,128)}) custom-call(f32[3,4,8,128]{3,2,1,0:T(8,128)} %base_in.1, f32[3072,128]{1,0:T(8,128)} %bitcast.2), custom_call_target="tpu_custom_call" | custom-call | tf_op jit(solution)/shard_map/pallas_call | solution.py:320
  27.7 7.7 %shard_map.42 = (f32[32,12,8,128]{3,2,1,0:T(8,128)}, f32[32,32]{1,0:T(8,128)}) custom-call(f32[32,32]{1,0:T(8,128)} %get-tuple-element.6.gram, bf16[12,64,1024]{2,1,0:T(8,128)(2,1)} %get-tuple-element.7.pieces), custom_call_target="tpu_custom_call" | custom-call | tf_op jit(solution)/shard_map/pallas_call | solution.py:347
